TPU v7x, 32 devices: a whole 2x2x4 slice. The times are simulated.
32 devices in a mesh: rows: 8 (over z, y), chan: 4 (over x, core).
Axes of the slice: x: 2, y: 2, z: 4, core: 2. Of those that a mesh axis runs over, the one named last changes fastest.
Arguments:
- radiances: float32 [16, 16384], P('chan', 'rows'), may hold values from -6 to 6
- band: int32 [16384, 1], P('rows'), may hold values from 0 to 7; in each aligned block of 2048 rows (0 to 2047, 2048 to 4095, ...) at most 512 rows name the same one
- row_in_band: int32 [16384], P('rows'), may hold values from 0 to 3
- column: int32 [16384], P('rows'), may hold values from 0 to 1439
Outputs:
- cell_count: int32 [32, 1440], P('rows')
- cell_mean: float32 [16, 32, 1440], P('chan', 'rows')
- cell_var: float32 [16, 32, 1440], P('chan', 'rows')
- cell_spread: float32 [32, 1440], P('rows')
- departure: float32 [16, 16384], P('chan', 'rows')
Inputs may be any that keep to these rules, and one draw needn't show every extreme that they name: Within each aligned block of 2048 observations (one scan-time shard) no band is named by more than 512 observations, and in some blocks one band is named by exactly 512.
All inputs are finite; a program needn't handle non-finite values.
Results may differ from a plain program's by a relative error of at most 0.0003.
Values sent between devices are 32-bit elements.
A program may use at most 64 MiB of HBM per device.

v0:
```python
import math
import jax
import jax.numpy as jnp
from jax import lax
from jax.sharding import PartitionSpec as P

CHAN = 16
COLS = 1440
ROWS_DEV = 4


def slot_ranks(dest, nrows):
    obs_dev = dest.shape[0]
    width = math.gcd(obs_dev, 128)
    nblock = obs_dev // width
    owners = jnp.arange(nrows, dtype=jnp.int32)
    hot = (dest[None, :] == owners[:, None]).astype(jnp.bfloat16).reshape(nrows, nblock, width)
    upper = (
        lax.broadcasted_iota(jnp.int32, (width, width), 0)
        <= lax.broadcasted_iota(jnp.int32, (width, width), 1)
    ).astype(jnp.bfloat16)
    inner = jnp.einsum("nbk,kj->nbj", hot, upper, preferred_element_type=jnp.float32)
    hot_float = hot.astype(jnp.float32)
    totals = jnp.sum(hot_float, axis=2)
    before = jnp.cumsum(totals, axis=1) - totals
    ranks = jnp.sum(hot_float * (inner + before[:, :, None]), axis=0).reshape(obs_dev) - 1.0
    return ranks.astype(jnp.int32)


def split_pair(values):
    high = lax.optimization_barrier(values.astype(jnp.bfloat16))
    low = (values - high.astype(jnp.float32)).astype(jnp.bfloat16)
    return (high, low)


def split_three(values):
    high = lax.optimization_barrier(values.astype(jnp.bfloat16))
    rest = values - high.astype(jnp.float32)
    middle = lax.optimization_barrier(rest.astype(jnp.bfloat16))
    low = (rest - middle.astype(jnp.float32)).astype(jnp.bfloat16)
    return (high, middle, low)


def grid_lookup(table, lat_index, col_index):
    fields, nlat, ncol = table.shape
    total = lat_index.shape[0]
    width = math.gcd(total, 2048)
    flat = table.reshape(fields * nlat, ncol)
    lat_iota = jnp.arange(nlat, dtype=jnp.int32)
    col_iota = jnp.arange(ncol, dtype=jnp.int32)

    def look_turn(turn, result):
        start = turn * width
        lat_part = lax.dynamic_slice_in_dim(lat_index, start, width, 0)
        col_part = lax.dynamic_slice_in_dim(col_index, start, width, 0)
        col_hot = (col_iota[:, None] == col_part[None, :]).astype(jnp.float32)
        picked = jnp.dot(
            flat, col_hot, precision=lax.Precision.HIGHEST, preferred_element_type=jnp.float32
        ).reshape(fields, nlat, width)
        lat_hot = (lat_iota[:, None] == lat_part[None, :]).astype(jnp.float32)
        found = jnp.sum(picked * lat_hot[None], axis=1)
        return lax.dynamic_update_slice_in_dim(result, found, start, 1)

    return lax.fori_loop(0, total // width, look_turn, jnp.zeros((fields, total), jnp.float32))


def body(radiances, band, row_in_band, column):
    nrows = lax.axis_size("rows")
    chan_dev, obs_dev = radiances.shape
    cap = 2 * obs_dev // nrows
    total_slots = nrows * cap
    dest = band[:, 0]
    slot = dest * cap + slot_ranks(dest, nrows)
    rad_high, rad_middle, rad_low = split_three(radiances)
    payload = jnp.concatenate(
        [
            rad_high,
            rad_middle,
            rad_low,
            row_in_band[None, :].astype(jnp.bfloat16),
            (column // 64)[None, :].astype(jnp.bfloat16),
            (column % 64)[None, :].astype(jnp.bfloat16),
            jnp.ones((1, obs_dev), jnp.bfloat16),
        ],
        axis=0,
    )
    nload = payload.shape[0]
    span = math.gcd(total_slots, 1024)
    slot_iota = jnp.arange(span, dtype=jnp.int32)

    def pack_turn(turn, buffer):
        start = turn * span
        hot = (slot[:, None] == (start + slot_iota)[None, :]).astype(jnp.bfloat16)
        placed_part = jnp.dot(payload, hot, preferred_element_type=jnp.float32)
        return lax.dynamic_update_slice_in_dim(buffer, placed_part, start, 1)

    placed = lax.fori_loop(
        0, total_slots // span, pack_turn, jnp.zeros((nload, total_slots), jnp.float32)
    )
    sent_values = (
        placed[0:chan_dev] + placed[chan_dev : 2 * chan_dev] + placed[2 * chan_dev : 3 * chan_dev]
    )
    base = 3 * chan_dev
    sent_cell = jnp.where(
        placed[base + 3] > 0.5,
        placed[base] * COLS + placed[base + 1] * 64.0 + placed[base + 2],
        -1.0,
    )
    packed = jnp.concatenate([sent_values, sent_cell[None, :]], axis=0).reshape(
        chan_dev + 1, nrows, cap
    )
    arrived = lax.all_to_all(packed, "rows", split_axis=1, concat_axis=1, tiled=True).reshape(
        chan_dev + 1, total_slots
    )
    values = arrived[:chan_dev]
    cell = arrived[chan_dev].astype(jnp.int32)
    lat_local = jnp.where(cell >= 0, cell // COLS, -1)
    col_local = jnp.where(cell >= 0, cell % COLS, -1)
    value_high, value_low = split_pair(values)
    square_high, square_low = split_pair(values * values)
    features = jnp.concatenate(
        [jnp.ones((1, total_slots), jnp.bfloat16), value_high, value_low, square_high, square_low],
        axis=0,
    )
    nfeat = features.shape[0]
    row_hot = (lat_local[None, :] == jnp.arange(ROWS_DEV, dtype=jnp.int32)[:, None]).astype(
        jnp.bfloat16
    )
    left = (features[:, None, :] * row_hot[None, :, :]).reshape(nfeat * ROWS_DEV, total_slots)
    block = math.gcd(total_slots, 2048)
    turns = total_slots // block
    columns_all = jnp.arange(COLS, dtype=jnp.int32)

    def accumulate(turn, acc):
        start = turn * block
        part = lax.dynamic_slice_in_dim(left, start, block, 1)
        picked = lax.dynamic_slice_in_dim(col_local, start, block, 0)
        col_hot = (picked[:, None] == columns_all[None, :]).astype(jnp.bfloat16)
        return acc + jnp.dot(part, col_hot, preferred_element_type=jnp.float32)

    sums = lax.fori_loop(0, turns, accumulate, jnp.zeros((nfeat * ROWS_DEV, COLS), jnp.float32))
    sums = sums.reshape(nfeat, ROWS_DEV, COLS)
    count = sums[0]
    first = sums[1 : 1 + chan_dev] + sums[1 + chan_dev : 1 + 2 * chan_dev]
    second = sums[1 + 2 * chan_dev : 1 + 3 * chan_dev] + sums[1 + 3 * chan_dev :]
    denom = jnp.maximum(count, 1.0)[None]
    mean = first / denom
    var = jnp.maximum(second / denom - mean * mean, 0.0)
    spread = lax.psum(jnp.sum(var, axis=0), "chan")
    scale = lax.rsqrt(1.0 + spread / CHAN)
    fields = grid_lookup(jnp.concatenate([mean, scale[None]], axis=0), lat_local, col_local)
    shifted = (values - fields[:chan_dev]) * fields[chan_dev][None, :]
    returned = lax.all_to_all(
        shifted.reshape(chan_dev, nrows, cap), "rows", split_axis=1, concat_axis=1, tiled=True
    )
    returned_flat = returned.reshape(chan_dev, total_slots)

    def unplace(turn, result):
        start = turn * span
        hot = (slot[:, None] == (start + slot_iota)[None, :]).astype(jnp.float32)
        part = lax.dynamic_slice_in_dim(returned_flat, start, span, 1)
        return result + lax.dot_general(
            part,
            hot,
            (((1,), (1,)), ((), ())),
            precision=lax.Precision.HIGHEST,
            preferred_element_type=jnp.float32,
        )

    departure = lax.fori_loop(
        0, total_slots // span, unplace, jnp.zeros((chan_dev, obs_dev), jnp.float32)
    )
    return (count.astype(jnp.int32), mean, var, spread, departure)


def solution(mesh):
    in_specs = (P("chan", "rows"), P("rows", None), P("rows"), P("rows"))
    out_specs = (
        P("rows", None),
        P("chan", "rows", None),
        P("chan", "rows", None),
        P("rows", None),
        P("chan", "rows"),
    )
    return jax.shard_map(body, mesh=mesh, in_specs=in_specs, out_specs=out_specs, check_vma=False)
```

profile of v0, /device:TPU:0, one launch (start us, length us, event | category | flops | bytes accessed | tf_op | source)
XLA Modules:
  0.0 82.0 jit_solution(14672771929657307120)
XLA Ops:
  0.6 0.8 convert_element_type.110
  1.4 0.8 fusion.46
  2.2 0.8 subtract_convert_fusion.2
  2.9 0.7 fusion.50
  3.7 0.7 convert_element_type.115
  4.4 0.7 broadcast_multiply_fusion.1
  5.1 0.8 convert_reduce_fusion
  6.1 0.9 %fusion.39 = f32[16,128]{1,0:T(8,128)S(1)} fusion(f32[8,16]{1,0:T(8,128)S(1)} %sub.41, s32[16,128]{1,0:T(8,128)} %bitcast.49), kind=kOutput, calls=%fused_computation.36 | convolution fusion | flops 4323328 | bytes 16896 | tf_op jit(solution)/shard_map/nbk,kj->nbj/dot_general | solution.py:22
  7.2 5.7 %while.56 = (s32[]{:T(128)}, f32[16,4096]{1,0:T(8,128)S(1)}, s32[2048]{0:T(1024)S(1)}, bf16[16,2048]{1,0:T(8,128)(2,1)S(1)}, s32[]{:T(128)}, /*index=5*/s32[]{:T(128)}, s32[]{:T(128)}, s32[]{:T(128)}) while((s32[]{:T(128)}, f32[16,4096]{1,0:T(8,128)S(1)}, s32[2048]{0:T(1024)S(1)}, bf16[16,2048]{1,0:T(8,128)(2,1)S(1)}, s32[]{:T(128)}, ...), condition=%wide.region_4.5_spmd.clone, body=%wide.region_3.4_spmd.clone.sunk | while | flops 69207048 | bytes 147595 | solution.py:97
  7.2 1.4 %fusion.70 = f32[16,4096]{1,0:T(8,128)S(1)} fusion(f32[16,4096]{1,0:T(8,128)S(1)} %get-tuple-element.638, s32[]{:T(128)S(6)} %select_n.104, bf16[16,2048]{1,0:T(8,128)(2,1)S(1)} %get-tuple-element.648, s32[1024]{0:T(1024)S(1)} %iota_add_fusion.4, s32[2048]{0:T(1024)S(1)} %get-tuple-element.647), kind=kOutput, calls=%fused_computation.10.clone.1 | convolution fusion | flops 69206016 | bytes 143364 | tf_op jit(solution)/shard_map/while/body/eval_jaxpr/dot_general | solution.py:94
  8.6 1.4 %fusion.70 = f32[16,4096]{1,0:T(8,128)S(1)} fusion(f32[16,4096]{1,0:T(8,128)S(1)} %get-tuple-element.638, s32[]{:T(128)S(6)} %select_n.104, bf16[16,2048]{1,0:T(8,128)(2,1)S(1)} %get-tuple-element.648, s32[1024]{0:T(1024)S(1)} %iota_add_fusion.4, s32[2048]{0:T(1024)S(1)} %get-tuple-element.647), kind=kOutput, calls=%fused_computation.10.clone.1 | convolution fusion | flops 69206016 | bytes 143364 | tf_op jit(solution)/shard_map/while/body/eval_jaxpr/dot_general | solution.py:94
  10.0 1.4 %fusion.70 = f32[16,4096]{1,0:T(8,128)S(1)} fusion(f32[16,4096]{1,0:T(8,128)S(1)} %get-tuple-element.638, s32[]{:T(128)S(6)} %select_n.104, bf16[16,2048]{1,0:T(8,128)(2,1)S(1)} %get-tuple-element.648, s32[1024]{0:T(1024)S(1)} %iota_add_fusion.4, s32[2048]{0:T(1024)S(1)} %get-tuple-element.647), kind=kOutput, calls=%fused_computation.10.clone.1 | convolution fusion | flops 69206016 | bytes 143364 | tf_op jit(solution)/shard_map/while/body/eval_jaxpr/dot_general | solution.py:94
  11.4 1.4 %fusion.70 = f32[16,4096]{1,0:T(8,128)S(1)} fusion(f32[16,4096]{1,0:T(8,128)S(1)} %get-tuple-element.638, s32[]{:T(128)S(6)} %select_n.104, bf16[16,2048]{1,0:T(8,128)(2,1)S(1)} %get-tuple-element.648, s32[1024]{0:T(1024)S(1)} %iota_add_fusion.4, s32[2048]{0:T(1024)S(1)} %get-tuple-element.647), kind=kOutput, calls=%fused_computation.10.clone.1 | convolution fusion | flops 69206016 | bytes 143364 | tf_op jit(solution)/shard_map/while/body/eval_jaxpr/dot_general | solution.py:94
  12.9 0.7 pad_maximum_fusion
  13.6 7.3 %all-to-all-start = ((f32[5,8,512]{2,0,1:T(8,128)}), f32[5,8,512]{2,0,1:T(8,128)S(1)}, u32[]{:S(2)}, u32[]{:S(2)}) async-start(f32[5,8,512]{2,0,1:T(8,128)} %pad_maximum_fusion), calls=%async_computation | async-start | bytes 262144 | tf_op jit(solution)/shard_map/all_to_all | solution.py:112
  20.9 7.3 %all-to-all-done = f32[5,8,512]{2,0,1:T(8,128)S(1)} async-done(((f32[5,8,512]{2,0,1:T(8,128)}), f32[5,8,512]{2,0,1:T(8,128)S(1)}, u32[]{:S(2)}, u32[]{:S(2)}) %all-to-all-start) | async-done | bytes 81952 | tf_op jit(solution)/shard_map/all_to_all | solution.py:112
  29.6 5.4 %while.58 = (s32[]{:T(128)}, f32[68,1440]{1,0:T(8,128)S(1)}, bf16[68,4096]{1,0:T(8,128)(2,1)S(1)}, s32[4096]{0:T(1024)S(1)}, s32[]{:T(128)}, /*index=5*/s32[]{:T(128)}, s32[]{:T(128)}, s32[]{:T(128)}) while((s32[]{:T(128)}, f32[68,1440]{1,0:T(8,128)S(1)}, bf16[68,4096]{1,0:T(8,128)(2,1)S(1)}, s32[4096]{0:T(1024)S(1)}, s32[]{:T(128)}, ...), condition=%wide.region_6.7_spmd.clone, body=%wide.region_5.6_spmd.clone.sunk | while | flops 404225280 | bytes 1153685 | solution.py:141
  29.6 2.7 %fusion.75 = f32[68,1440]{1,0:T(8,128)S(1)} fusion(s32[2048]{0:T(1024)S(1)} %dynamic_slice.52, f32[68,1440]{1,0:T(8,128)S(1)} %get-tuple-element.662, bf16[68,4096]{1,0:T(8,128)(2,1)S(1)} %get-tuple-element.671, s32[]{:T(128)S(6)} %select_n.106, pred[]{:T(512)S(6)} %compare.9), kind=kOutput, calls=%fused_computation.23.clone.1 | convolution fusion | flops 404225280 | bytes 1137157 | tf_op jit(solution)/shard_map/while/body/eval_jaxpr/dot_general | solution.py:139
  32.3 2.7 %fusion.75 = f32[68,1440]{1,0:T(8,128)S(1)} fusion(s32[2048]{0:T(1024)S(1)} %dynamic_slice.52, f32[68,1440]{1,0:T(8,128)S(1)} %get-tuple-element.662, bf16[68,4096]{1,0:T(8,128)(2,1)S(1)} %get-tuple-element.671, s32[]{:T(128)S(6)} %select_n.106, pred[]{:T(512)S(6)} %compare.9), kind=kOutput, calls=%fused_computation.23.clone.1 | convolution fusion | flops 404225280 | bytes 1137157 | tf_op jit(solution)/shard_map/while/body/eval_jaxpr/dot_general | solution.py:139
  35.7 0.7 fusion.53
  36.5 10.3 %psum.7 = f32[4,1440]{1,0:T(4,128)S(1)} all-reduce(f32[4,1440]{1,0:T(4,128)S(1)} %get-tuple-element.508), channel_id=1, replica_groups=mesh['rows'=8,'chan'=4] {'chan'}, use_global_device_ids=true, to_apply=%region_8.9 | all-reduce | flops 5760 | bytes 46080 | tf_op jit(solution)/shard_map/psum | solution.py:149
  47.3 8.0 %while.57 = (s32[]{:T(128)}, f32[5,4096]{1,0:T(8,128)S(1)}, s32[4096]{0:T(1024)S(1)}, f32[20,1440]{1,0:T(8,128)S(1)}, s32[4096]{0:T(1024)S(1)}, /*index=5*/s32[]{:T(128)}, s32[]{:T(128)}, s32[]{:T(128)}, s32[]{:T(128)}) while((s32[]{:T(128)}, f32[5,4096]{1,0:T(8,128)S(1)}, s32[4096]{0:T(1024)S(1)}, f32[20,1440]{1,0:T(8,128)S(1)}, ...), condition=%wide.region_11.12_spmd.clone, body=%wide.region_9.11_spmd.clone.sunk | while | flops 710825984 | bytes 1057431 | solution.py:64
  47.3 3.7 %fusion.72 = f32[20,2048]{1,0:T(8,128)S(1)} fusion(f32[20,1440]{1,0:T(8,128)S(1)} %get-tuple-element.698, s32[2048]{0:T(1024)S(1)} %dynamic_slice.49), kind=kOutput, calls=%fused_computation.15.clone.1 | convolution fusion | flops 710737920 | bytes 287232 | tf_op jit(solution)/shard_map/while/body/eval_jaxpr/dot_general | solution.py:57
  51.3 3.7 %fusion.72 = f32[20,2048]{1,0:T(8,128)S(1)} fusion(f32[20,1440]{1,0:T(8,128)S(1)} %get-tuple-element.698, s32[2048]{0:T(1024)S(1)} %dynamic_slice.49), kind=kOutput, calls=%fused_computation.15.clone.1 | convolution fusion | flops 710737920 | bytes 287232 | tf_op jit(solution)/shard_map/while/body/eval_jaxpr/dot_general | solution.py:57
  55.3 0.6 subtract_multiply_fusion
  56.0 3.3 %all-to-all-start.1 = ((f32[4,8,512]{2,0,1:T(4,128)}), f32[4,8,512]{2,0,1:T(4,128)S(1)}, u32[]{:S(2)}, u32[]{:S(2)}) async-start(f32[4,8,512]{2,0,1:T(4,128)} %bitcast.11), calls=%async_computation.1 | async-start | bytes 131072 | tf_op jit(solution)/shard_map/all_to_all | solution.py:153
  59.4 6.8 %all-to-all-done.1 = f32[4,8,512]{2,0,1:T(4,128)S(1)} async-done(((f32[4,8,512]{2,0,1:T(4,128)}), f32[4,8,512]{2,0,1:T(4,128)S(1)}, u32[]{:S(2)}, u32[]{:S(2)}) %all-to-all-start.1) | async-done | bytes 65568 | tf_op jit(solution)/shard_map/all_to_all | solution.py:153
  66.2 15.2 %while.59 = (s32[]{:T(128)}, f32[4,2048]{1,0:T(4,128)S(1)}, f32[4,4096]{1,0:T(4,128)S(1)}, s32[2048]{0:T(1024)S(1)}, s32[]{:T(128)}, /*index=5*/s32[]{:T(128)}, s32[]{:T(128)}, s32[]{:T(128)}) while((s32[]{:T(128)}, f32[4,2048]{1,0:T(4,128)S(1)}, f32[4,4096]{1,0:T(4,128)S(1)}, s32[2048]{0:T(1024)S(1)}, s32[]{:T(128)}, ...), condition=%wide.region_13.14_spmd.clone, body=%wide.region_12.13_spmd.clone.sunk | while | flops 102777864 | bytes 98453 | solution.py:170
  66.2 3.8 %fusion.78 = f32[4,2048]{1,0:T(4,128)S(1)} fusion(s32[1024]{0:T(1024)S(1)} %iota_add_fusion.5, s32[2048]{0:T(1024)S(1)} %get-tuple-element.723, f32[4,2048]{1,0:T(4,128)S(1)} %get-tuple-element.713, f32[4,4096]{1,0:T(4,128)S(1)} %get-tuple-element.722, s32[]{:T(128)S(6)} %select_n.107, pred[]{:T(512)S(6)} %compare.10), kind=kOutput, calls=%fused_computation.30.clone.1 | convolution fusion | flops 102776832 | bytes 94213 | tf_op jit(solution)/shard_map/while/body/eval_jaxpr/dot_general | solution.py:162
  70.0 3.8 %fusion.78 = f32[4,2048]{1,0:T(4,128)S(1)} fusion(s32[1024]{0:T(1024)S(1)} %iota_add_fusion.5, s32[2048]{0:T(1024)S(1)} %get-tuple-element.723, f32[4,2048]{1,0:T(4,128)S(1)} %get-tuple-element.713, f32[4,4096]{1,0:T(4,128)S(1)} %get-tuple-element.722, s32[]{:T(128)S(6)} %select_n.107, pred[]{:T(512)S(6)} %compare.10), kind=kOutput, calls=%fused_computation.30.clone.1 | convolution fusion | flops 102776832 | bytes 94213 | tf_op jit(solution)/shard_map/while/body/eval_jaxpr/dot_general | solution.py:162
  73.8 3.8 %fusion.78 = f32[4,2048]{1,0:T(4,128)S(1)} fusion(s32[1024]{0:T(1024)S(1)} %iota_add_fusion.5, s32[2048]{0:T(1024)S(1)} %get-tuple-element.723, f32[4,2048]{1,0:T(4,128)S(1)} %get-tuple-element.713, f32[4,4096]{1,0:T(4,128)S(1)} %get-tuple-element.722, s32[]{:T(128)S(6)} %select_n.107, pred[]{:T(512)S(6)} %compare.10), kind=kOutput, calls=%fused_computation.30.clone.1 | convolution fusion | flops 102776832 | bytes 94213 | tf_op jit(solution)/shard_map/while/body/eval_jaxpr/dot_general | solution.py:162
  77.6 3.8 %fusion.78 = f32[4,2048]{1,0:T(4,128)S(1)} fusion(s32[1024]{0:T(1024)S(1)} %iota_add_fusion.5, s32[2048]{0:T(1024)S(1)} %get-tuple-element.723, f32[4,2048]{1,0:T(4,128)S(1)} %get-tuple-element.713, f32[4,4096]{1,0:T(4,128)S(1)} %get-tuple-element.722, s32[]{:T(128)S(6)} %select_n.107, pred[]{:T(512)S(6)} %compare.10), kind=kOutput, calls=%fused_computation.30.clone.1 | convolution fusion | flops 102776832 | bytes 94213 | tf_op jit(solution)/shard_map/while/body/eval_jaxpr/dot_general | solution.py:162
  (64 shorter events, 4.0 us)
Async XLA Ops:
  13.6 14.7 %all-to-all-start = ((f32[5,8,512]{2,0,1:T(8,128)}), f32[5,8,512]{2,0,1:T(8,128)S(1)}, u32[]{:S(2)}, u32[]{:S(2)}) async-start(f32[5,8,512]{2,0,1:T(8,128)} %pad_maximum_fusion), calls=%async_computation | async-start | bytes 262144 | tf_op jit(solution)/shard_map/all_to_all | solution.py:112
  36.4 10.4 %copy-start = (f32[4,4,1440]{2,1,0:T(4,128)}, f32[4,4,1440]{2,1,0:T(4,128)S(1)}, u32[]{:S(2)}) copy-start(f32[4,4,1440]{2,1,0:T(4,128)S(1)} %get-tuple-element.510) | copy-start | bytes 276484
  46.7 0.6 copy-start.1
  56.0 10.2 %all-to-all-start.1 = ((f32[4,8,512]{2,0,1:T(4,128)}), f32[4,8,512]{2,0,1:T(4,128)S(1)}, u32[]{:S(2)}, u32[]{:S(2)}) async-start(f32[4,8,512]{2,0,1:T(4,128)} %bitcast.11), calls=%async_computation.1 | async-start | bytes 131072 | tf_op jit(solution)/shard_map/all_to_all | solution.py:153
  81.4 0.6 copy-start.2
where the time goes:
time: 82.7 us; the launch traced here: 82 us
  matrix products  34.5 us (42%)
  waiting for transfers between devices  14.2 us (17%)
  starting transfers between devices  10.7 us (13%)
  blocking collectives  10.3 us (12%)
  other arithmetic  9.1 us (11%)
  local copies, waits for them, and re-layouts  2.18 us (3%)
  between operations  0.93 us (1%)
    dot_general x4, matrix products, unplace(): lax.dot_general(part, hot, (((1,), (1,)), ((), ())), precision=lax.Precis...  15.1 us
    psum x1, blocking collectives, body(): spread = lax.psum(jnp.sum(var, axis=0), 'chan')  10.3 us
    dot_general x2, matrix products, look_turn(): jnp.dot(flat, col_hot, precision=lax.Precision.HIGHEST, preferred_element...  7.49 us
    all_to_all x1, waiting for transfers between devices, body(): lax.all_to_all(packed, 'rows', split_axis=1, concat_axis=1, tiled=True)  7.34 us
    all_to_all x1, starting transfers between devices, body(): lax.all_to_all(packed, 'rows', split_axis=1, concat_axis=1, tiled=True)  7.31 us
    all_to_all x1, waiting for transfers between devices, body(): lax.all_to_all(shifted.reshape(chan_dev, nrows, cap), 'rows', split_axis=...  6.83 us
    dot_general x4, matrix products, pack_turn(): placed_part = jnp.dot(payload, hot, preferred_element_type=jnp.float32)  5.63 us
    dot_general x2, matrix products, accumulate(): return acc + jnp.dot(part, col_hot, preferred_element_type=jnp.float32)  5.3 us
  transfers between devices with their start and end apart: 2, of which 2 were waited for; matrix products, arithmetic and copies ran while one was open for 0% of the time, Pallas kernels for 0%

commit v1 on v0

--- a/solution.py
+++ b/solution.py
@@ -146,7 +146,7 @@
     denom = jnp.maximum(count, 1.0)[None]
     mean = first / denom
     var = jnp.maximum(second / denom - mean * mean, 0.0)
-    spread = lax.psum(jnp.sum(var, axis=0), "chan")
+    spread = jnp.sum(lax.all_gather(jnp.sum(var, axis=0), "chan"), axis=0)
     scale = lax.rsqrt(1.0 + spread / CHAN)
     fields = grid_lookup(jnp.concatenate([mean, scale[None]], axis=0), lat_local, col_local)
     shifted = (values - fields[:chan_dev]) * fields[chan_dev][None, :]

time: 82.7 us -> 77.8 us (0.941)
  blocking collectives: 10.3 us -> 5.31 us
    psum x1 -> x0, blocking collectives: 10.3 us -> none  [body(): spread = lax.psum(jnp.sum(var, axis=0), 'chan')]
    all_gather x0 -> x1, blocking collectives: none -> 5.31 us  [body(): spread = jnp.sum(lax.all_gather(jnp.sum(var, axis=0), 'chan'), axis=0)]
where the time goes in v1:
time: 77.8 us; the launch traced here: 77.1 us
  matrix products  34.5 us (44%)
  waiting for transfers between devices  14.2 us (18%)
  starting transfers between devices  10.7 us (14%)
  other arithmetic  9.13 us (12%)
  blocking collectives  5.31 us (7%)
  local copies, waits for them, and re-layouts  2.18 us (3%)
  between operations  0.93 us (1%)
    dot_general x4, matrix products, unplace(): lax.dot_general(part, hot, (((1,), (1,)), ((), ())), precision=lax.Precis...  15.1 us
    dot_general x2, matrix products, look_turn(): jnp.dot(flat, col_hot, precision=lax.Precision.HIGHEST, preferred_element...  7.49 us
    all_to_all x1, waiting for transfers between devices, body(): lax.all_to_all(packed, 'rows', split_axis=1, concat_axis=1, tiled=True)  7.34 us
    all_to_all x1, starting transfers between devices, body(): lax.all_to_all(packed, 'rows', split_axis=1, concat_axis=1, tiled=True)  7.31 us
    all_to_all x1, waiting for transfers between devices, body(): lax.all_to_all(shifted.reshape(chan_dev, nrows, cap), 'rows', split_axis=...  6.83 us
    dot_general x4, matrix products, pack_turn(): placed_part = jnp.dot(payload, hot, preferred_element_type=jnp.float32)  5.63 us
    all_gather x1, blocking collectives, body(): spread = jnp.sum(lax.all_gather(jnp.sum(var, axis=0), 'chan'), axis=0)  5.31 us
    dot_general x2, matrix products, accumulate(): return acc + jnp.dot(part, col_hot, preferred_element_type=jnp.float32)  5.3 us
  transfers between devices with their start and end apart: 2, of which 2 were waited for; matrix products, arithmetic and copies ran while one was open for 0% of the time, Pallas kernels for 0%

profile of v1, /device:TPU:0, one launch (start us, length us, event | category | flops | bytes accessed | tf_op | source)
XLA Modules:
  0.0 77.1 jit_solution(3056551716962871957)
XLA Ops:
  0.6 0.8 convert_element_type.110
  1.4 0.8 fusion.46
  2.2 0.8 %subtract_convert_fusion.2 = bf16[4,2048]{1,0:T(4,128)(2,1)S(1)} fusion(bf16[4,2048]{1,0:T(4,128)(2,1)S(1)} %fusion.46, f32[4,2048]{1,0:T(4,128)} %param.12, bf16[4,2048]{1,0:T(4,128)(2,1)S(1)} %convert_element_type.110), kind=kLoop, calls=%fused_computation.60 | loop fusion | flops 40960 | bytes 81920 | tf_op jit(solution)/shard_map/convert_element_type | solution.py:40
  2.9 0.7 fusion.50
  3.7 0.7 convert_element_type.115
  4.4 0.7 broadcast_multiply_fusion.1
  5.1 0.8 %convert_reduce_fusion = f32[8,16]{1,0:T(8,128)S(1)} fusion(s32[16,128]{1,0:T(8,128)} %bitcast.50), kind=kLoop, calls=%fused_computation.44 | loop fusion | flops 65408 | bytes 8704 | tf_op jit(solution)/shard_map/reduce_sum | solution.py:24
  6.1 0.9 %fusion.39 = f32[16,128]{1,0:T(8,128)S(1)} fusion(f32[8,16]{1,0:T(8,128)S(1)} %sub.41, s32[16,128]{1,0:T(8,128)} %bitcast.51), kind=kOutput, calls=%fused_computation.36 | convolution fusion | flops 4323328 | bytes 16896 | tf_op jit(solution)/shard_map/nbk,kj->nbj/dot_general | solution.py:22
  7.2 5.7 %while.56 = (s32[]{:T(128)}, f32[16,4096]{1,0:T(8,128)S(1)}, s32[2048]{0:T(1024)S(1)}, bf16[16,2048]{1,0:T(8,128)(2,1)S(1)}, s32[]{:T(128)}, /*index=5*/s32[]{:T(128)}, s32[]{:T(128)}, s32[]{:T(128)}) while((s32[]{:T(128)}, f32[16,4096]{1,0:T(8,128)S(1)}, s32[2048]{0:T(1024)S(1)}, bf16[16,2048]{1,0:T(8,128)(2,1)S(1)}, s32[]{:T(128)}, ...), condition=%wide.region_4.5_spmd.clone, body=%wide.region_3.4_spmd.clone.sunk | while | flops 69207048 | bytes 147595 | solution.py:97
  7.2 1.4 %fusion.70 = f32[16,4096]{1,0:T(8,128)S(1)} fusion(f32[16,4096]{1,0:T(8,128)S(1)} %get-tuple-element.638, s32[]{:T(128)S(6)} %select_n.104, bf16[16,2048]{1,0:T(8,128)(2,1)S(1)} %get-tuple-element.648, s32[1024]{0:T(1024)S(1)} %iota_add_fusion.4, s32[2048]{0:T(1024)S(1)} %get-tuple-element.647), kind=kOutput, calls=%fused_computation.10.clone.1 | convolution fusion | flops 69206016 | bytes 143364 | tf_op jit(solution)/shard_map/while/body/eval_jaxpr/dot_general | solution.py:94
  8.6 1.4 %fusion.70 = f32[16,4096]{1,0:T(8,128)S(1)} fusion(f32[16,4096]{1,0:T(8,128)S(1)} %get-tuple-element.638, s32[]{:T(128)S(6)} %select_n.104, bf16[16,2048]{1,0:T(8,128)(2,1)S(1)} %get-tuple-element.648, s32[1024]{0:T(1024)S(1)} %iota_add_fusion.4, s32[2048]{0:T(1024)S(1)} %get-tuple-element.647), kind=kOutput, calls=%fused_computation.10.clone.1 | convolution fusion | flops 69206016 | bytes 143364 | tf_op jit(solution)/shard_map/while/body/eval_jaxpr/dot_general | solution.py:94
  10.0 1.4 %fusion.70 = f32[16,4096]{1,0:T(8,128)S(1)} fusion(f32[16,4096]{1,0:T(8,128)S(1)} %get-tuple-element.638, s32[]{:T(128)S(6)} %select_n.104, bf16[16,2048]{1,0:T(8,128)(2,1)S(1)} %get-tuple-element.648, s32[1024]{0:T(1024)S(1)} %iota_add_fusion.4, s32[2048]{0:T(1024)S(1)} %get-tuple-element.647), kind=kOutput, calls=%fused_computation.10.clone.1 | convolution fusion | flops 69206016 | bytes 143364 | tf_op jit(solution)/shard_map/while/body/eval_jaxpr/dot_general | solution.py:94
  11.4 1.4 %fusion.70 = f32[16,4096]{1,0:T(8,128)S(1)} fusion(f32[16,4096]{1,0:T(8,128)S(1)} %get-tuple-element.638, s32[]{:T(128)S(6)} %select_n.104, bf16[16,2048]{1,0:T(8,128)(2,1)S(1)} %get-tuple-element.648, s32[1024]{0:T(1024)S(1)} %iota_add_fusion.4, s32[2048]{0:T(1024)S(1)} %get-tuple-element.647), kind=kOutput, calls=%fused_computation.10.clone.1 | convolution fusion | flops 69206016 | bytes 143364 | tf_op jit(solution)/shard_map/while/body/eval_jaxpr/dot_general | solution.py:94
  12.9 0.7 pad_maximum_fusion
  13.6 7.3 %all-to-all-start = ((f32[5,8,512]{2,0,1:T(8,128)}), f32[5,8,512]{2,0,1:T(8,128)S(1)}, u32[]{:S(2)}, u32[]{:S(2)}) async-start(f32[5,8,512]{2,0,1:T(8,128)} %pad_maximum_fusion), calls=%async_computation | async-start | bytes 262144 | tf_op jit(solution)/shard_map/all_to_all | solution.py:112
  20.9 7.3 %all-to-all-done = f32[5,8,512]{2,0,1:T(8,128)S(1)} async-done(((f32[5,8,512]{2,0,1:T(8,128)}), f32[5,8,512]{2,0,1:T(8,128)S(1)}, u32[]{:S(2)}, u32[]{:S(2)}) %all-to-all-start) | async-done | bytes 81952 | tf_op jit(solution)/shard_map/all_to_all | solution.py:112
  29.6 5.4 %while.58 = (s32[]{:T(128)}, f32[68,1440]{1,0:T(8,128)S(1)}, bf16[68,4096]{1,0:T(8,128)(2,1)S(1)}, s32[4096]{0:T(1024)S(1)}, s32[]{:T(128)}, /*index=5*/s32[]{:T(128)}, s32[]{:T(128)}, s32[]{:T(128)}) while((s32[]{:T(128)}, f32[68,1440]{1,0:T(8,128)S(1)}, bf16[68,4096]{1,0:T(8,128)(2,1)S(1)}, s32[4096]{0:T(1024)S(1)}, s32[]{:T(128)}, ...), condition=%wide.region_6.7_spmd.clone, body=%wide.region_5.6_spmd.clone.sunk | while | flops 404225280 | bytes 1153685 | solution.py:141
  29.6 2.7 %fusion.75 = f32[68,1440]{1,0:T(8,128)S(1)} fusion(s32[2048]{0:T(1024)S(1)} %dynamic_slice.52, f32[68,1440]{1,0:T(8,128)S(1)} %get-tuple-element.662, bf16[68,4096]{1,0:T(8,128)(2,1)S(1)} %get-tuple-element.671, s32[]{:T(128)S(6)} %select_n.106, pred[]{:T(512)S(6)} %compare.9), kind=kOutput, calls=%fused_computation.23.clone.1 | convolution fusion | flops 404225280 | bytes 1137157 | tf_op jit(solution)/shard_map/while/body/eval_jaxpr/dot_general | solution.py:139
  32.3 2.7 %fusion.75 = f32[68,1440]{1,0:T(8,128)S(1)} fusion(s32[2048]{0:T(1024)S(1)} %dynamic_slice.52, f32[68,1440]{1,0:T(8,128)S(1)} %get-tuple-element.662, bf16[68,4096]{1,0:T(8,128)(2,1)S(1)} %get-tuple-element.671, s32[]{:T(128)S(6)} %select_n.106, pred[]{:T(512)S(6)} %compare.9), kind=kOutput, calls=%fused_computation.23.clone.1 | convolution fusion | flops 404225280 | bytes 1137157 | tf_op jit(solution)/shard_map/while/body/eval_jaxpr/dot_general | solution.py:139
  35.7 0.7 fusion.53
  36.5 5.3 %all-gather.1 = f32[4,4,1440]{2,1,0:T(4,128)S(1)} all-gather(f32[1,4,1440]{2,1,0:T(4,128)S(1)} %bitcast.43), channel_id=2, replica_groups=mesh['rows'=8,'chan'=4] {'chan'}, dimensions={0}, use_global_device_ids=true | all-gather | bytes 115200 | tf_op jit(solution)/shard_map/all_gather | solution.py:149
  42.4 8.0 %while.57 = (s32[]{:T(128)}, f32[5,4096]{1,0:T(8,128)S(1)}, s32[4096]{0:T(1024)S(1)}, f32[20,1440]{1,0:T(8,128)S(1)}, s32[4096]{0:T(1024)S(1)}, /*index=5*/s32[]{:T(128)}, s32[]{:T(128)}, s32[]{:T(128)}, s32[]{:T(128)}) while((s32[]{:T(128)}, f32[5,4096]{1,0:T(8,128)S(1)}, s32[4096]{0:T(1024)S(1)}, f32[20,1440]{1,0:T(8,128)S(1)}, ...), condition=%wide.region_11.12_spmd.clone, body=%wide.region_9.11_spmd.clone.sunk | while | flops 710825984 | bytes 1057431 | solution.py:64
  42.4 3.7 %fusion.72 = f32[20,2048]{1,0:T(8,128)S(1)} fusion(f32[20,1440]{1,0:T(8,128)S(1)} %get-tuple-element.698, s32[2048]{0:T(1024)S(1)} %dynamic_slice.49), kind=kOutput, calls=%fused_computation.15.clone.1 | convolution fusion | flops 710737920 | bytes 287232 | tf_op jit(solution)/shard_map/while/body/eval_jaxpr/dot_general | solution.py:57
  46.4 3.7 %fusion.72 = f32[20,2048]{1,0:T(8,128)S(1)} fusion(f32[20,1440]{1,0:T(8,128)S(1)} %get-tuple-element.698, s32[2048]{0:T(1024)S(1)} %dynamic_slice.49), kind=kOutput, calls=%fused_computation.15.clone.1 | convolution fusion | flops 710737920 | bytes 287232 | tf_op jit(solution)/shard_map/while/body/eval_jaxpr/dot_general | solution.py:57
  50.4 0.6 subtract_multiply_fusion
  51.1 3.3 %all-to-all-start.1 = ((f32[4,8,512]{2,0,1:T(4,128)}), f32[4,8,512]{2,0,1:T(4,128)S(1)}, u32[]{:S(2)}, u32[]{:S(2)}) async-start(f32[4,8,512]{2,0,1:T(4,128)} %bitcast.12), calls=%async_computation.1 | async-start | bytes 131072 | tf_op jit(solution)/shard_map/all_to_all | solution.py:153
  54.4 6.8 %all-to-all-done.1 = f32[4,8,512]{2,0,1:T(4,128)S(1)} async-done(((f32[4,8,512]{2,0,1:T(4,128)}), f32[4,8,512]{2,0,1:T(4,128)S(1)}, u32[]{:S(2)}, u32[]{:S(2)}) %all-to-all-start.1) | async-done | bytes 65568 | tf_op jit(solution)/shard_map/all_to_all | solution.py:153
  61.3 15.2 %while.59 = (s32[]{:T(128)}, f32[4,2048]{1,0:T(4,128)S(1)}, f32[4,4096]{1,0:T(4,128)S(1)}, s32[2048]{0:T(1024)S(1)}, s32[]{:T(128)}, /*index=5*/s32[]{:T(128)}, s32[]{:T(128)}, s32[]{:T(128)}) while((s32[]{:T(128)}, f32[4,2048]{1,0:T(4,128)S(1)}, f32[4,4096]{1,0:T(4,128)S(1)}, s32[2048]{0:T(1024)S(1)}, s32[]{:T(128)}, ...), condition=%wide.region_13.14_spmd.clone, body=%wide.region_12.13_spmd.clone.sunk | while | flops 102777864 | bytes 98453 | solution.py:170
  61.3 3.8 %fusion.78 = f32[4,2048]{1,0:T(4,128)S(1)} fusion(s32[1024]{0:T(1024)S(1)} %iota_add_fusion.5, s32[2048]{0:T(1024)S(1)} %get-tuple-element.723, f32[4,2048]{1,0:T(4,128)S(1)} %get-tuple-element.713, f32[4,4096]{1,0:T(4,128)S(1)} %get-tuple-element.722, s32[]{:T(128)S(6)} %select_n.107, pred[]{:T(512)S(6)} %compare.10), kind=kOutput, calls=%fused_computation.30.clone.1 | convolution fusion | flops 102776832 | bytes 94213 | tf_op jit(solution)/shard_map/while/body/eval_jaxpr/dot_general | solution.py:162
  65.1 3.8 %fusion.78 = f32[4,2048]{1,0:T(4,128)S(1)} fusion(s32[1024]{0:T(1024)S(1)} %iota_add_fusion.5, s32[2048]{0:T(1024)S(1)} %get-tuple-element.723, f32[4,2048]{1,0:T(4,128)S(1)} %get-tuple-element.713, f32[4,4096]{1,0:T(4,128)S(1)} %get-tuple-element.722, s32[]{:T(128)S(6)} %select_n.107, pred[]{:T(512)S(6)} %compare.10), kind=kOutput, calls=%fused_computation.30.clone.1 | convolution fusion | flops 102776832 | bytes 94213 | tf_op jit(solution)/shard_map/while/body/eval_jaxpr/dot_general | solution.py:162
  68.9 3.8 %fusion.78 = f32[4,2048]{1,0:T(4,128)S(1)} fusion(s32[1024]{0:T(1024)S(1)} %iota_add_fusion.5, s32[2048]{0:T(1024)S(1)} %get-tuple-element.723, f32[4,2048]{1,0:T(4,128)S(1)} %get-tuple-element.713, f32[4,4096]{1,0:T(4,128)S(1)} %get-tuple-element.722, s32[]{:T(128)S(6)} %select_n.107, pred[]{:T(512)S(6)} %compare.10), kind=kOutput, calls=%fused_computation.30.clone.1 | convolution fusion | flops 102776832 | bytes 94213 | tf_op jit(solution)/shard_map/while/body/eval_jaxpr/dot_general | solution.py:162
  72.7 3.8 %fusion.78 = f32[4,2048]{1,0:T(4,128)S(1)} fusion(s32[1024]{0:T(1024)S(1)} %iota_add_fusion.5, s32[2048]{0:T(1024)S(1)} %get-tuple-element.723, f32[4,2048]{1,0:T(4,128)S(1)} %get-tuple-element.713, f32[4,4096]{1,0:T(4,128)S(1)} %get-tuple-element.722, s32[]{:T(128)S(6)} %select_n.107, pred[]{:T(512)S(6)} %compare.10), kind=kOutput, calls=%fused_computation.30.clone.1 | convolution fusion | flops 102776832 | bytes 94213 | tf_op jit(solution)/shard_map/while/body/eval_jaxpr/dot_general | solution.py:162
  (65 shorter events, 4.1 us)
Async XLA Ops:
  13.6 14.7 %all-to-all-start = ((f32[5,8,512]{2,0,1:T(8,128)}), f32[5,8,512]{2,0,1:T(8,128)S(1)}, u32[]{:S(2)}, u32[]{:S(2)}) async-start(f32[5,8,512]{2,0,1:T(8,128)} %pad_maximum_fusion), calls=%async_computation | async-start | bytes 262144 | tf_op jit(solution)/shard_map/all_to_all | solution.py:112
  36.4 5.5 %copy-start = (f32[4,4,1440]{2,1,0:T(4,128)}, f32[4,4,1440]{2,1,0:T(4,128)S(1)}, u32[]{:S(2)}) copy-start(f32[4,4,1440]{2,1,0:T(4,128)S(1)} %get-tuple-element.510) | copy-start | bytes 276484
  41.8 0.6 copy-start.1
  51.1 10.2 %all-to-all-start.1 = ((f32[4,8,512]{2,0,1:T(4,128)}), f32[4,8,512]{2,0,1:T(4,128)S(1)}, u32[]{:S(2)}, u32[]{:S(2)}) async-start(f32[4,8,512]{2,0,1:T(4,128)} %bitcast.12), calls=%async_computation.1 | async-start | bytes 131072 | tf_op jit(solution)/shard_map/all_to_all | solution.py:153
  76.5 0.6 copy-start.2
